TPU v7x, 32 devices: a whole 2x2x4 slice. The times are simulated.
32 devices in a mesh: ctx: 8 (over y, x, core), exp: 4 (over z).
Axes of the slice: x: 2, y: 2, z: 4, core: 2. Of those that a mesh axis runs over, the one named last changes fastest.
Arguments:
- mixer_input: bfloat16 [8192, 4096], P('ctx', 'exp'), may hold values from -6 to 6
- scale_exponent: int32 [64, 64], P('ctx', 'exp'), may hold values from -1 to 1
- step_size: float32 [64, 8192], P('exp', 'ctx'), may hold values from 0.25 to 1
- decay_log: float32 [64, 8192], P('exp', 'ctx'), may hold values from -1.2 to 0
- state_input: bfloat16 [8192, 128], P('ctx'), may hold values from -6 to 6
- state_output: bfloat16 [8192, 128], P('ctx'), may hold values from -0.5 to 0.5
- skip_gain: float32 [64], P('exp'), may hold values from 0.5 to 1.5
- gate_input: bfloat16 [8192, 4096], P('ctx', 'exp'), may hold values from -6 to 6
- norm_gain: float32 [4096], P('exp'), may hold values from 0.25 to 1.75
- up_weight: bfloat16 [4096, 3072], P('ctx', 'exp'), may hold values from -0.09375 to 0.09375
- down_weight: bfloat16 [3072, 4096], P('exp', 'ctx'), may hold values from -0.15625 to 0.15625
- expert_slot: int32 [8192], P('ctx'), may hold values from 0 to 256, as said below
- gate_prob: float32 [8192], P('ctx'), may hold values from 0.2 to 1
Outputs:
- layer_out: bfloat16 [8192, 4096], P('ctx', 'exp')
Inputs may be any that keep to these rules, and one draw needn't show every extreme that they name: `expert_slot`: within each aligned block of 1024 tokens, the tokens routed to the expert carry the distinct slots 0 to k - 1 for some k of at most 256, and all other tokens carry 256; in some block k equals 256.
All inputs are finite; a program needn't handle non-finite values.
Results may differ from a plain program's by a relative error of at most 0.0085.
Values may be sent and summed in bfloat16 or wider, within the bound.
No kernel may reach another device: no remote copies, remote signals or barrier semaphores. Data moves between devices by JAX's collectives and lax.ppermute only.
A program may use at most 128 MiB of HBM per device.

v0:
```python
import jax
import jax.numpy as jnp
from jax import lax
from jax.sharding import PartitionSpec as P

P_SIZE = 64
BLK = 128
CAP = 256
highest = lax.Precision.HIGHEST


def local_scan(x_in, step_size, decay_log, b_rows, c_rows):
    length, head_count, head_width = x_in.shape
    blocks = length // BLK
    x_blocks = x_in.reshape(blocks, BLK, head_count, head_width)
    b_blocks = b_rows.reshape(blocks, BLK, b_rows.shape[1])
    c_blocks = c_rows.reshape(blocks, BLK, c_rows.shape[1])
    step_blocks = step_size.reshape(head_count, blocks, BLK)
    cumulative = jnp.cumsum(decay_log.reshape(head_count, blocks, BLK), axis=2)
    scores = jnp.einsum("bin,bjn->bij", c_blocks, b_blocks, precision=highest)
    causal = jnp.arange(BLK)[:, None] >= jnp.arange(BLK)[None, :]
    spread = jnp.where(causal, cumulative[:, :, :, None] - cumulative[:, :, None, :], -jnp.inf)
    mixing = jnp.exp(spread) * scores[None] * step_blocks[:, :, None, :]
    inner_part = jnp.einsum("hbij,bjhp->bihp", mixing, x_blocks, precision=highest)
    tail_decay = jnp.exp(cumulative[:, :, -1:] - cumulative) * step_blocks
    block_state = jnp.einsum(
        "hbj,bjn,bjhp->bhnp", tail_decay, b_blocks, x_blocks, precision=highest
    )
    totals = cumulative[:, :, -1]

    def carry_on(running, block_items):
        block_total, block_end = block_items
        return (jnp.exp(block_total)[:, None, None] * running + block_end, running)

    running, entering = lax.scan(
        carry_on, jnp.zeros(block_state.shape[1:], jnp.float32), (totals.T, block_state)
    )
    carried = jnp.einsum(
        "bin,hbi,bhnp->bihp", c_blocks, jnp.exp(cumulative), entering, precision=highest
    )
    offsets = jnp.cumsum(totals, axis=1) - totals
    growth = jnp.exp(offsets[:, :, None] + cumulative)
    return (inner_part + carried, running, jnp.sum(totals, axis=1), c_blocks, growth)


def body(
    mixer_input,
    scale_exponent,
    step_size,
    decay_log,
    state_input,
    state_output,
    skip_gain,
    gate_input,
    norm_gain,
    up_weight,
    down_weight,
    expert_slot,
    gate_prob,
):
    length = mixer_input.shape[0]
    head_count = skip_gain.shape[0]
    blocks = length // BLK
    factor = jnp.exp2(scale_exponent.astype(jnp.float32))
    x_in = (
        mixer_input.astype(jnp.float32).reshape(blocks, BLK, head_count, P_SIZE)
        * factor[:, None, :, None]
    ).reshape(length, head_count, P_SIZE)
    b_rows = state_input.astype(jnp.float32)
    c_rows = state_output.astype(jnp.float32)
    local_out, end_state, total_log, c_blocks, growth = local_scan(
        x_in, step_size, decay_log, b_rows, c_rows
    )
    log_totals = lax.all_gather(total_log[None, :], "ctx", axis=0, tiled=True)
    before = jnp.cumsum(log_totals, axis=0) - log_totals
    position = lax.axis_index("ctx")
    own_prior = lax.dynamic_index_in_dim(before, position, 0, keepdims=False)
    shard_piece = lax.all_gather(
        end_state[None].astype(jnp.bfloat16), "ctx", axis=0, tiled=True
    ).astype(jnp.float32)
    row_count = shard_piece.shape[0]
    row_ids = jnp.arange(row_count, dtype=jnp.int32)
    decay_gap = jnp.minimum(own_prior[None, :] - before - log_totals, 0.0)
    weight = jnp.where((row_ids < position)[:, None], jnp.exp(decay_gap), 0.0)
    start_state = jnp.zeros_like(end_state) + jnp.einsum(
        "kh,khnp->hnp", weight, shard_piece, precision=highest
    )
    handed = jnp.einsum("bin,hbi,hnp->bihp", c_blocks, growth, start_state, precision=highest)
    mixer_out = (local_out + handed).reshape(length, head_count, P_SIZE) + skip_gain[
        None, :, None
    ] * x_in
    gated_out = mixer_out * jax.nn.silu(
        gate_input.astype(jnp.float32).reshape(length, head_count, P_SIZE)
    )
    inverse_rms = lax.rsqrt(jnp.mean(gated_out * gated_out, axis=2, keepdims=True) + 1e-05)
    normed = (
        (gated_out * inverse_rms * norm_gain.reshape(head_count, P_SIZE))
        .reshape(length, head_count * P_SIZE)
        .astype(jnp.bfloat16)
    )
    places = jnp.arange(CAP, dtype=jnp.int32)[:, None] == expert_slot[None, :]
    picker = places.astype(jnp.bfloat16)
    dispatched = jnp.dot(picker, normed, preferred_element_type=jnp.float32).astype(jnp.bfloat16)
    full_features = lax.all_gather(dispatched, "exp", axis=1, tiled=True)
    up_act = jnp.dot(
        full_features,
        lax.all_gather(up_weight, "ctx", axis=0, tiled=True),
        preferred_element_type=jnp.float32,
    )
    hidden = jax.nn.silu(up_act).astype(jnp.bfloat16)
    terms = jnp.dot(
        hidden,
        lax.all_gather(down_weight, "ctx", axis=1, tiled=True),
        preferred_element_type=jnp.float32,
    )
    own_sums = lax.psum_scatter(
        terms.astype(jnp.bfloat16), "exp", scatter_dimension=1, tiled=True
    ).astype(jnp.float32)
    selector = places.astype(jnp.float32)
    expert_tok = lax.dot_general(selector, own_sums, (((0,), (0,)), ((), ())), precision=highest)
    return (normed.astype(jnp.float32) + gate_prob[:, None] * expert_tok).astype(jnp.bfloat16)


def solution(mesh):
    in_specs = (
        P("ctx", "exp"),
        P("ctx", "exp"),
        P("exp", "ctx"),
        P("exp", "ctx"),
        P("ctx", None),
        P("ctx", None),
        P("exp"),
        P("ctx", "exp"),
        P("exp"),
        P("ctx", "exp"),
        P("exp", "ctx"),
        P("ctx"),
        P("ctx"),
    )
    out_specs = P("ctx", "exp")
    return jax.shard_map(body, mesh=mesh, in_specs=in_specs, out_specs=out_specs, check_vma=False)
```

profile of v0, /device:TPU:0, one launch (start us, length us, event | category | flops | bytes accessed | tf_op | source)
XLA Modules:
  0.0 375.8 jit_solution(6003521538814983370)
XLA Ops:
  7.4 4.5 %reduce_window_sum.33 = f32[16,8,128]{2,1,0:T(8,128)S(1)} reduce-window(f32[16,8,128]{2,1,0:T(8,128)S(1)} %bitcast.107, f32[]{:T(128)} %constant.28.clone.1), window={size=1x1x128 pad=0_0x0_0x127_0}, to_apply=%region_0.0 | reduce-window | flops 2080768 | bytes 131076 | tf_op jit(solution)/shard_map/jit(cumsum)/reduce_window_sum | solution.py:19
  14.6 6.8 %reshape.91 = f32[8,128,16,64]{3,2,1,0:T(8,128)} reshape(bf16[1024,1024]{1,0:T(8,128)(2,1)} %param.15) | data formatting | bytes 6291456 | tf_op jit(solution)/shard_map/reshape | solution.py:66
  21.4 7.2 %copy.74 = f32[8,128,16,64]{1,3,2,0:T(8,128)} copy(f32[8,128,16,64]{3,2,1,0:T(8,128)} %reshape.91) | data formatting | bytes 8388608 | tf_op jit(solution)/shard_map/reshape | solution.py:66
  28.5 6.4 %fusion.20 = f32[8,16,128,64]{2,3,1,0:T(8,128)} fusion(bf16[8,128,128,1]{2,1,3,0:T(8,128)(2,1)S(1)} %bitcast.102, f32[8,128,16,64]{1,3,2,0:T(8,128)} %copy.74, f32[8,128,16]{1,2,0:T(8,128)S(1)} %copy.81, f32[8,16]{1,0:T(8,128)S(1)} %multiply_exponential_fusion), kind=kOutput, calls=%fused_computation.31 | convolution fusion | flops 1612709888 | bytes 8716800 | tf_op jit(solution)/shard_map/hbj,bjn,bjhp->bhnp/dot_general | solution.py:26
  35.0 21.8 %while.13 = (s32[]{:T(128)}, f32[16,128,64]{2,1,0:T(8,128)S(1)}, f32[8,16,128,64]{3,2,1,0:T(8,128)}, f32[8,16]{1,0:T(8,128)S(1)}, f32[8,16,128,64]{2,3,1,0:T(8,128)}, /*index=5*/s32[]{:T(128)}, s32[]{:T(128)}) while((s32[]{:T(128)}, f32[16,128,64]{2,1,0:T(8,128)S(1)}, f32[8,16,128,64]{3,2,1,0:T(8,128)}, f32[8,16]{1,0:T(8,128)S(1)}, ...), condition=%wide.region_2.3_spmd.clone, body=%wide.region_1.2_spmd.clone.sunk | while | flops 524291 | bytes 5243680 | solution.py:35
  59.4 15.6 %all-reduce = f32[128]{0:T(128)S(1)} all-reduce(f32[128]{0:T(128)S(1)} %dynamic-update-slice), channel_id=2, replica_groups=mesh['ctx'=8,'exp'=4] {'ctx'}, use_global_device_ids=true, to_apply=%add | all-reduce | flops 128 | bytes 1024
  75.1 6.8 %reshape.93 = f32[8,128,16,64]{3,2,1,0:T(8,128)} reshape(bf16[1024,1024]{1,0:T(8,128)(2,1)} %param.22) | data formatting | bytes 6291456 | tf_op jit(solution)/shard_map/reshape | solution.py:93
  81.9 7.2 %copy.94 = f32[8,128,16,64]{1,3,2,0:T(8,128)} copy(f32[8,128,16,64]{3,2,1,0:T(8,128)} %reshape.93) | data formatting | bytes 8388608 | tf_op jit(solution)/shard_map/reshape | solution.py:93
  89.2 2.5 mul.135
  91.6 5.4 %copy.90 = f32[1024,1024]{1,0:T(8,128)} copy(f32[1024,1024]{0,1:T(8,128)} %bitcast.99) | data formatting | bytes 8388608 | tf_op jit(solution)/shard_map/mul | solution.py:66
  97.6 12.1 %fusion.35 = f32[8,16,64,128]{3,2,1,0:T(8,128)} fusion(f32[8,16,128,64]{3,2,1,0:T(8,128)} %get-tuple-element.33, bf16[8,128,128,1]{2,1,3,0:T(8,128)(2,1)S(1)} %bitcast.96), kind=kOutput, calls=%fused_computation.60 | convolution fusion | flops 1610612736 | bytes 8650752 | tf_op jit(solution)/shard_map/bin,hbi,bhnp->bihp/dot_general | solution.py:38
  109.8 18.0 %fusion.2 = f32[8,16,64,128]{3,2,1,0:T(8,128)} fusion(f32[16,8,128]{2,0,1:T(8,128)S(1)} %copy_bitcast_fusion.2, f32[8,128,128]{2,1,0:T(8,128)S(1)} %fusion.34, f32[16,8,128]{2,0,1:T(8,128)S(1)} %copy.75, pred[128,128]{1,0:T(8,128)(4,1)S(1)} %iota_compare_fusion.3, f32[8,128,16,64]{1,3,2,0:T(8,128)S(1)} %copy-done.2, f32[8,16]{1,0:T(8,128)S(1)} %multiply_exponential_fusion), kind=kOutput, calls=%fused_computation.6 | convolution fusion | flops 1620049920 | bytes 9060864 | tf_op jit(solution)/shard_map/hbij,bjhp->bihp/dot_general | solution.py:24
  129.8 9.3 %multiply_reduce_fusion.1 = (f32[8,128,16]{1,2,0:T(8,128)S(1)}, f32[8,128,16,64]{1,3,2,0:T(8,128)}) fusion(f32[8,128,16,64]{1,3,2,0:T(8,128)} %copy.94, f32[8,128,16,64]{1,3,2,0:T(8,128)} %copy.74, f32[16]{0:T(128)S(1)} %copy-done.9, f32[8,16]{1,0:T(8,128)S(1)} %multiply_exponential_fusion, bf16[8,128,128,1]{2,1,3,0:T(8,128)(2,1)S(1)} %bitcast.97, ...), kind=kOutput, calls=%fused_computation.20 | convolution fusion | flops 1625276416 | bytes 21955136 | tf_op jit(solution)/shard_map/bin,hbi,hnp->bihp/dot_general | solution.py:88
  139.1 7.1 %copy.110 = f32[8,128,16,64]{3,2,1,0:T(8,128)} copy(f32[8,128,16,64]{1,3,2,0:T(8,128)} %get-tuple-element.89) | data formatting | bytes 8388608 | tf_op jit(solution)/shard_map/reshape | solution.py:89
  146.3 7.6 %reshape.92 = f32[1024,1024]{1,0:T(8,128)} reshape(f32[8,128,16,64]{3,2,1,0:T(8,128)} %copy.110) | data formatting | bytes 8388608 | tf_op jit(solution)/shard_map/reshape | solution.py:89
  153.9 2.5 mul.146
  156.4 5.5 %copy.96 = f32[1024,1024]{1,0:T(8,128)} copy(f32[1024,1024]{0,1:T(8,128)} %bitcast.100) | data formatting | bytes 8388608 | tf_op jit(solution)/shard_map/mul | solution.py:97
  161.9 6.6 %multiply_convert_fusion = bf16[1024,1024]{1,0:T(8,128)(2,1)S(1)} fusion(f32[1024,1024]{1,0:T(8,128)} %copy.96, f32[1024,1024]{1,0:T(8,128)} %reshape.92, f32[1024,1024]{1,0:T(8,128)} %copy.90, f32[1024]{0:T(1024)S(1)} %copy-done.8, f32[1024]{0:T(1024)S(1)} %mul.131, bf16[1024,1024]{1,0:T(8,128)(2,1)S(1)} %copy-done.3, bf16[1024,1024]{1,0:T(8,128)(2,1)} %param.15), kind=kLoop, calls=%fused_computation.19 | loop fusion | flops 13631488 | bytes 18882560 | tf_op jit(solution)/shard_map/convert_element_type | solution.py:99
  172.8 43.8 %all-gather.7.cloned.1.call-done = bf16[256,4096]{1,0:T(8,128)(2,1)} async-done(((bf16[256,1024]{1,0:T(8,128)(2,1)}), bf16[256,4096]{1,0:T(8,128)(2,1)}) %all-gather.7.cloned.1.call-update) | async-done | bytes 2097168 | tf_op jit(solution)/shard_map/all_gather | solution.py:104
  216.6 47.3 %all-gather.11.cloned.1.call-done = bf16[768,4096]{1,0:T(8,128)(2,1)} async-done(((bf16[768,512]{1,0:T(8,128)(2,1)}), bf16[768,4096]{1,0:T(8,128)(2,1)}) %all-gather.11.cloned.1.call-update) | async-done | bytes 6291472 | tf_op jit(solution)/shard_map/all_gather | solution.py:113
  263.9 47.2 %all-gather.9.cloned.1.call-done = bf16[4096,768]{1,0:T(8,128)(2,1)} async-done(((bf16[512,768]{1,0:T(8,128)(2,1)}), bf16[4096,768]{1,0:T(8,128)(2,1)}) %all-gather.9.cloned.1.call-update) | async-done | bytes 6291472 | tf_op jit(solution)/shard_map/all_gather | solution.py:107
  311.1 11.1 %convolution_convert_fusion = bf16[256,4096]{1,0:T(8,128)(2,1)} fusion(bf16[768,4096]{1,0:T(8,128)(2,1)} %all-gather.11.cloned.1.call-done, bf16[256,4096]{1,0:T(8,128)(2,1)} %all-gather.7.cloned.1.call-done, bf16[4096,768]{1,0:T(8,128)(2,1)} %all-gather.9.cloned.1.call-done), kind=kOutput, calls=%fused_computation.12 | convolution fusion | flops 3223257088 | bytes 16777216 | tf_op jit(solution)/shard_map/dot_general | solution.py:111
  322.2 43.8 %reduce-scatter.2.cloned.1.call-done = bf16[256,1024]{1,0:T(8,128)(2,1)} async-done(((bf16[256,4096]{1,0:T(8,128)(2,1)}), bf16[256,1024]{1,0:T(8,128)(2,1)}) %reduce-scatter.2.cloned.1.call-update) | async-done | bytes 524304 | tf_op jit(solution)/shard_map/reduce_scatter | solution.py:116
  366.0 3.3 add_convert_fusion
  (114 shorter events, 34.0 us)
Async XLA Ops:
  6.5 90.8 %copy-start = (bf16[1024,128]{1,0:T(8,128)(2,1)S(1)}, bf16[1024,128]{1,0:T(8,128)(2,1)}, u32[]{:S(2)}) copy-start(bf16[1024,128]{1,0:T(8,128)(2,1)} %param.20) | copy-start | bytes 786436
  6.5 121.2 %all-gather.13.cloned.1.call-start = ((), (), s32[]{:S(2)}) async-start(), calls=%async_computation.5 | async-start | bytes 2359296 | tf_op jit(solution)/shard_map/all_gather | solution.py:78
  21.4 7.2 %copy-start.6 = (bf16[1024,128]{1,0:T(8,128)(2,1)S(1)}, bf16[1024,128]{1,0:T(8,128)(2,1)}, u32[]{:S(2)}) copy-start(bf16[1024,128]{1,0:T(8,128)(2,1)} %param.19) | copy-start | bytes 786436
  35.0 22.9 %copy-start.12 = (u32[32]{0:T(128)S(1)}, u32[32]{0:T(128)}, u32[]{:S(2)}) copy-start(u32[32]{0:T(128)} %constant.54) | copy-start | bytes 388
  57.7 158.9 %all-gather.7.cloned.1.call-start = ((), (), s32[]{:S(2)}) async-start(), calls=%async_computation.1 | async-start | bytes 2621440 | tf_op jit(solution)/shard_map/all_gather | solution.py:104
  91.6 5.4 %copy-start.9 = (f32[16]{0:T(128)S(1)}, f32[16]{0:T(128)}, u32[]{:S(2)}) copy-start(f32[16]{0:T(128)} %param.21) | copy-start | bytes 196
  91.6 5.7 %copy-start.7 = (f32[16,1024]{1,0:T(8,128)S(1)}, f32[16,1024]{1,0:T(8,128)}, u32[]{:S(2)}) copy-start(f32[16,1024]{1,0:T(8,128)} %param.17) | copy-start | bytes 196612
  97.6 12.1 %copy-start.2 = (f32[8,128,16,64]{1,3,2,0:T(8,128)S(1)}, f32[8,128,16,64]{1,3,2,0:T(8,128)}, u32[]{:S(2)}) copy-start(f32[8,128,16,64]{1,3,2,0:T(8,128)} %copy.74) | copy-start | bytes 12582916
  156.4 5.5 %copy-start.3 = (bf16[1024,1024]{1,0:T(8,128)(2,1)S(1)}, bf16[1024,1024]{1,0:T(8,128)(2,1)}, u32[]{:S(2)}) copy-start(bf16[1024,1024]{1,0:T(8,128)(2,1)} %param.22) | copy-start | bytes 6291460
  156.4 5.5 %copy-start.8 = (f32[1024]{0:T(1024)S(1)}, f32[1024]{0:T(1024)}, u32[]{:S(2)}) copy-start(f32[1024]{0:T(1024)} %param.23) | copy-start | bytes 12292
  161.9 7.9 %copy-start.10 = (s32[1024]{0:T(1024)S(1)}, s32[1024]{0:T(1024)}, u32[]{:S(2)}) copy-start(s32[1024]{0:T(1024)} %param.26) | copy-start | bytes 12292
  168.5 1.3 copy-start.4
  171.4 92.5 %all-gather.11.cloned.1.call-start = ((), (), s32[]{:S(2)}) async-start(), calls=%async_computation.3 | async-start | bytes 7077888 | tf_op jit(solution)/shard_map/all_gather | solution.py:113
  172.2 138.9 %all-gather.9.cloned.1.call-start = ((), (), s32[]{:S(2)}) async-start(), calls=%async_computation.2 | async-start | bytes 7077888 | tf_op jit(solution)/shard_map/all_gather | solution.py:107
  172.7 193.2 %copy-start.5 = (bf16[1024,1024]{1,0:T(8,128)(2,1)S(1)}, bf16[1024,1024]{1,0:T(8,128)(2,1)}, u32[]{:S(2)}) copy-start(bf16[1024,1024]{1,0:T(8,128)(2,1)} %copy-done.4) | copy-start | bytes 6291460
  172.8 193.2 %copy-start.11 = (f32[1024]{0:T(1024)S(1)}, f32[1024]{0:T(1024)}, u32[]{:S(2)}) copy-start(f32[1024]{0:T(1024)} %param.27) | copy-start | bytes 12292
  172.8 193.2 %reduce-scatter.2.cloned.1.call-start = ((), (), s32[]{:S(2)}) async-start(), calls=%async_computation.4 | async-start | bytes 2621440 | tf_op jit(solution)/shard_map/reduce_scatter | solution.py:116
  311.1 58.2 %copy-start.1 = (bf16[1024,128]{1,0:T(8,128)(2,1)S(1)}, bf16[1024,128]{1,0:T(8,128)(2,1)}, u32[]{:S(2)}) copy-start(bf16[1024,128]{1,0:T(8,128)(2,1)} %param.20) | copy-start | bytes 786436
Sparse Core Ops, SparseCore 0:
  57.8 30.5 all-gather.12
  171.5 45.0 all-gather.6
  218.5 45.3 all-gather.10
  265.6 45.3 all-gather.8
  322.3 43.6 reduce-scatter.1
where the time goes:
time: 377 us; the launch traced here: 376 us
  waiting for transfers between devices  183 us (49%)
  local copies, waits for them, and re-layouts  75.8 us (20%)
  matrix products  62 us (16%)
  other arithmetic  24.6 us (7%)
  blocking collectives  15.6 us (4%)
  between operations  14 us (4%)
    all_gather x1, waiting for transfers between devices, body(): lax.all_gather(down_weight, 'ctx', axis=1, tiled=True)  47.3 us
    all_gather x1, waiting for transfers between devices, body(): lax.all_gather(up_weight, 'ctx', axis=0, tiled=True)  47.2 us
    all_gather x1, waiting for transfers between devices, body(): full_features = lax.all_gather(dispatched, 'exp', axis=1, tiled=True)  43.8 us
    reduce_scatter x1, waiting for transfers between devices, body(): lax.psum_scatter(terms.astype(jnp.bfloat16), 'exp', scatter_dimension=1,...  43.8 us
    dot_general x1, matrix products, local_scan(): jnp.einsum('hbij,bjhp->bihp', mixing, x_blocks, precision=highest)  18 us
    unnamed x1, blocking collectives  15.6 us
    reshape x2, local copies, waits for them, and re-layouts, body(): (local_out + handed).reshape(length, head_count, P_SIZE)  14.8 us
    reshape x2, local copies, waits for them, and re-layouts, body(): gate_input.astype(jnp.float32).reshape(length, head_count, P_SIZE)  14 us
  transfers between devices with their start and end apart: 5, of which 4 were waited for; matrix products, arithmetic and copies ran while one was open for 14% of the time, Pallas kernels for 0%

commit v1 on v0

--- a/solution.py
+++ b/solution.py
@@ -101,7 +101,9 @@
     places = jnp.arange(CAP, dtype=jnp.int32)[:, None] == expert_slot[None, :]
     picker = places.astype(jnp.bfloat16)
     dispatched = jnp.dot(picker, normed, preferred_element_type=jnp.float32).astype(jnp.bfloat16)
-    full_features = lax.all_gather(dispatched, "exp", axis=1, tiled=True)
+    full_features = jnp.concatenate(
+        lax.all_to_all(jnp.stack([dispatched] * lax.axis_size("exp")), "exp", 0, 0), axis=1
+    )
     up_act = jnp.dot(
         full_features,
         lax.all_gather(up_weight, "ctx", axis=0, tiled=True),

time: 377 us -> 289 us (0.77)
  waiting for transfers between devices: 183 us -> 43.5 us
  blocking collectives: 15.6 us -> 67.4 us
    all_to_all x0 -> x1, blocking collectives: none -> 52 us  [body(): lax.all_to_all(jnp.stack([dispatched] * lax.axis_size('exp')), 'exp', 0, 0)]
    all_gather x1, waiting for transfers between devices: 47.3 us -> 0.01 us  [body(): lax.all_gather(down_weight, 'ctx', axis=1, tiled=True)]
    all_gather x1, waiting for transfers between devices: 47.2 us -> 0.01 us  [body(): lax.all_gather(up_weight, 'ctx', axis=0, tiled=True)]
    all_gather x1 -> x0, waiting for transfers between devices: 43.8 us -> none  [body(): full_features = lax.all_gather(dispatched, 'exp', axis=1, tiled=True)]
  transfers between devices with their start and end apart: 5 -> 4, of which waited for: 4 -> 1; matrix products, arithmetic and copies ran while one was open for 14% -> 33% of each run, Pallas kernels for 0% -> 0%
where the time goes in v1:
time: 289 us; the launch traced here: 288 us
  local copies, waits for them, and re-layouts  74.7 us (26%)
  blocking collectives  67.4 us (23%)
  matrix products  62.1 us (21%)
  waiting for transfers between devices  43.5 us (15%)
  other arithmetic  25.6 us (9%)
  between operations  14 us (5%)
    all_to_all x1, blocking collectives, body(): lax.all_to_all(jnp.stack([dispatched] * lax.axis_size('exp')), 'exp', 0, 0)  52 us
    reduce_scatter x1, waiting for transfers between devices, body(): lax.psum_scatter(terms.astype(jnp.bfloat16), 'exp', scatter_dimension=1,...  42.1 us
    dot_general x1, matrix products, local_scan(): jnp.einsum('hbij,bjhp->bihp', mixing, x_blocks, precision=highest)  18 us
    unnamed x1, blocking collectives  15.5 us
    reshape x2, local copies, waits for them, and re-layouts, body(): (local_out + handed).reshape(length, head_count, P_SIZE)  14.9 us
    reshape x2, local copies, waits for them, and re-layouts, body(): mixer_input.astype(jnp.float32).reshape(blocks, BLK, head_count, P_SIZE)  14 us
    dot_general x1, matrix products, local_scan(): jnp.einsum('bin,hbi,bhnp->bihp', c_blocks, jnp.exp(cumulative), entering,...  12.5 us
    reshape x2, local copies, waits for them, and re-layouts, body(): gate_input.astype(jnp.float32).reshape(length, head_count, P_SIZE)  11.7 us
  transfers between devices with their start and end apart: 4, of which 1 were waited for; matrix products, arithmetic and copies ran while one was open for 33% of the time, Pallas kernels for 0%

profile of v1, /device:TPU:0, one launch (start us, length us, event | category | flops | bytes accessed | tf_op | source)
XLA Modules:
  0.0 287.8 jit_solution(13571739520266292853)
XLA Ops:
  7.4 4.5 %reduce_window_sum.33 = f32[16,8,128]{2,1,0:T(8,128)S(1)} reduce-window(f32[16,8,128]{2,1,0:T(8,128)S(1)} %bitcast.111, f32[]{:T(128)} %constant.28.clone.1), window={size=1x1x128 pad=0_0x0_0x127_0}, to_apply=%region_0.0 | reduce-window | flops 2080768 | bytes 131076 | tf_op jit(solution)/shard_map/jit(cumsum)/reduce_window_sum | solution.py:19
  15.1 6.8 %reshape.101 = f32[8,128,16,64]{3,2,1,0:T(8,128)} reshape(bf16[1024,1024]{1,0:T(8,128)(2,1)} %param.15) | data formatting | bytes 6291456 | tf_op jit(solution)/shard_map/reshape | solution.py:66
  21.9 7.2 %copy.76 = f32[8,128,16,64]{1,3,2,0:T(8,128)} copy(f32[8,128,16,64]{3,2,1,0:T(8,128)} %reshape.101) | data formatting | bytes 8388608 | tf_op jit(solution)/shard_map/reshape | solution.py:66
  29.1 6.4 %fusion.20 = f32[8,16,128,64]{2,3,1,0:T(8,128)} fusion(bf16[8,128,128,1]{2,1,3,0:T(8,128)(2,1)S(1)} %bitcast.106, f32[8,128,16,64]{1,3,2,0:T(8,128)} %copy.76, f32[8,128,16]{1,2,0:T(8,128)S(1)} %copy.83, f32[8,16]{1,0:T(8,128)S(1)} %multiply_exponential_fusion), kind=kOutput, calls=%fused_computation.31 | convolution fusion | flops 1612709888 | bytes 8716800 | tf_op jit(solution)/shard_map/hbj,bjn,bjhp->bhnp/dot_general | solution.py:26
  35.5 21.8 %while.13 = (s32[]{:T(128)}, f32[16,128,64]{2,1,0:T(8,128)S(1)}, f32[8,16,128,64]{3,2,1,0:T(8,128)}, f32[8,16]{1,0:T(8,128)S(1)}, f32[8,16,128,64]{2,3,1,0:T(8,128)}, /*index=5*/s32[]{:T(128)}, s32[]{:T(128)}) while((s32[]{:T(128)}, f32[16,128,64]{2,1,0:T(8,128)S(1)}, f32[8,16,128,64]{3,2,1,0:T(8,128)}, f32[8,16]{1,0:T(8,128)S(1)}, ...), condition=%wide.region_2.3_spmd.clone, body=%wide.region_1.2_spmd.clone.sunk | while | flops 524291 | bytes 5243680 | solution.py:35
  61.4 15.5 %all-reduce = f32[128]{0:T(128)S(1)} all-reduce(f32[128]{0:T(128)S(1)} %dynamic-update-slice), channel_id=2, replica_groups=mesh['ctx'=8,'exp'=4] {'ctx'}, use_global_device_ids=true, to_apply=%add | all-reduce | flops 128 | bytes 1024
  77.9 4.5 %reshape.103 = f32[8,128,16,64]{3,2,1,0:T(8,128)} reshape(bf16[1024,1024]{1,0:T(8,128)(2,1)S(1)} %copy-done.3) | data formatting | bytes 6291456 | tf_op jit(solution)/shard_map/reshape | solution.py:93
  82.4 7.2 %copy.96 = f32[8,128,16,64]{1,3,2,0:T(8,128)} copy(f32[8,128,16,64]{3,2,1,0:T(8,128)} %reshape.103) | data formatting | bytes 8388608 | tf_op jit(solution)/shard_map/reshape | solution.py:93
  89.7 2.5 mul.135
  92.2 5.4 %copy.92 = f32[1024,1024]{1,0:T(8,128)} copy(f32[1024,1024]{0,1:T(8,128)} %bitcast.102) | data formatting | bytes 8388608 | tf_op jit(solution)/shard_map/mul | solution.py:66
  98.2 12.5 %fusion.35 = f32[8,16,64,128]{3,2,1,0:T(8,128)} fusion(f32[8,16,128,64]{3,2,1,0:T(8,128)} %get-tuple-element.33, bf16[8,128,128,1]{2,1,3,0:T(8,128)(2,1)S(1)} %bitcast.99), kind=kOutput, calls=%fused_computation.60 | convolution fusion | flops 1610612736 | bytes 8650752 | tf_op jit(solution)/shard_map/bin,hbi,bhnp->bihp/dot_general | solution.py:38
  110.6 18.0 %fusion.2 = f32[8,16,64,128]{3,2,1,0:T(8,128)} fusion(f32[16,8,128]{2,0,1:T(8,128)S(1)} %copy_bitcast_fusion.2, f32[8,128,128]{2,1,0:T(8,128)S(1)} %fusion.34, f32[16,8,128]{2,0,1:T(8,128)S(1)} %copy.77, pred[128,128]{1,0:T(8,128)(4,1)S(1)} %iota_compare_fusion.3, f32[8,128,16,64]{1,3,2,0:T(8,128)S(1)} %copy-done.2, f32[8,16]{1,0:T(8,128)S(1)} %multiply_exponential_fusion), kind=kOutput, calls=%fused_computation.6 | convolution fusion | flops 1620049920 | bytes 9060864 | tf_op jit(solution)/shard_map/hbij,bjhp->bihp/dot_general | solution.py:24
  128.6 2.1 multiply_reduce_fusion
  130.8 9.6 %multiply_reduce_fusion.1 = (f32[8,128,16]{1,2,0:T(8,128)S(1)}, f32[8,128,16,64]{1,3,2,0:T(8,128)}) fusion(f32[8,128,16,64]{1,3,2,0:T(8,128)} %copy.96, f32[8,128,16,64]{1,3,2,0:T(8,128)} %copy.76, f32[16]{0:T(128)S(1)} %copy-done.10, f32[8,16]{1,0:T(8,128)S(1)} %multiply_exponential_fusion, bf16[8,128,128,1]{2,1,3,0:T(8,128)(2,1)S(1)} %bitcast.100, ...), kind=kOutput, calls=%fused_computation.20 | convolution fusion | flops 1625276416 | bytes 21955136 | tf_op jit(solution)/shard_map/bin,hbi,hnp->bihp/dot_general | solution.py:88
  140.3 7.2 %copy.113 = f32[8,128,16,64]{3,2,1,0:T(8,128)} copy(f32[8,128,16,64]{1,3,2,0:T(8,128)} %get-tuple-element.89) | data formatting | bytes 8388608 | tf_op jit(solution)/shard_map/reshape | solution.py:89
  147.5 7.7 %reshape.102 = f32[1024,1024]{1,0:T(8,128)} reshape(f32[8,128,16,64]{3,2,1,0:T(8,128)} %copy.113) | data formatting | bytes 8388608 | tf_op jit(solution)/shard_map/reshape | solution.py:89
  155.2 2.5 mul.146
  157.7 5.4 %copy.98 = f32[1024,1024]{1,0:T(8,128)} copy(f32[1024,1024]{0,1:T(8,128)} %bitcast.103) | data formatting | bytes 8388608 | tf_op jit(solution)/shard_map/mul | solution.py:97
  163.1 7.0 %multiply_convert_fusion = bf16[1024,1024]{1,0:T(8,128)(2,1)S(1)} fusion(f32[1024,1024]{1,0:T(8,128)} %copy.98, f32[1024,1024]{1,0:T(8,128)} %reshape.102, f32[1024,1024]{1,0:T(8,128)} %copy.92, f32[1024]{0:T(1024)S(1)} %copy-done.9, f32[1024]{0:T(1024)S(1)} %mul.131, bf16[1024,1024]{1,0:T(8,128)(2,1)S(1)} %copy-done.3, bf16[1024,1024]{1,0:T(8,128)(2,1)} %param.15), kind=kLoop, calls=%fused_computation.19 | loop fusion | flops 13631488 | bytes 18882560 | tf_op jit(solution)/shard_map/convert_element_type | solution.py:99
  170.1 1.3 copy-done.4
  172.5 52.0 %all_to_all.5 = bf16[4,256,1024]{1,2,0:T(8,128)(2,1)} all-to-all(bf16[4,256,1024]{1,2,0:T(8,128)(2,1)S(1)} %stack.2), channel_id=1, replica_groups=mesh['ctx'=8,'exp'=4] {'exp'}, dimensions={0} | all-to-all | bytes 4194304 | tf_op jit(solution)/shard_map/all_to_all | solution.py:105
  224.5 11.4 %convolution_convert_fusion = bf16[256,4096]{1,0:T(8,128)(2,1)} fusion(bf16[768,4096]{1,0:T(8,128)(2,1)} %all-gather.8.cloned.1.call-done, bf16[256,4096]{0,1:T(8,128)(2,1)} %bitcast.105, bf16[4096,768]{1,0:T(8,128)(2,1)} %all-gather.6.cloned.1.call-done), kind=kOutput, calls=%fused_computation.12 | convolution fusion | flops 3223257088 | bytes 16777216 | tf_op jit(solution)/shard_map/dot_general | solution.py:113
  235.9 42.1 %reduce-scatter.2.cloned.1.call-done = bf16[256,1024]{1,0:T(8,128)(2,1)} async-done(((bf16[256,4096]{1,0:T(8,128)(2,1)}), bf16[256,1024]{1,0:T(8,128)(2,1)}) %reduce-scatter.2.cloned.1.call-update) | async-done | bytes 524304 | tf_op jit(solution)/shard_map/reduce_scatter | solution.py:118
  278.0 3.3 %add_convert_fusion = bf16[1024,1024]{1,0:T(8,128)(2,1)} fusion(bf16[1024,1024]{1,0:T(8,128)(2,1)S(1)} %copy-done.5, bf16[256,1024]{1,0:T(8,128)(2,1)} %reduce-scatter.2.cloned.1.call-done, f32[1024]{0:T(1024)S(1)} %copy-done.12, s32[1024]{0:T(1024)S(1)} %copy-done.11), kind=kOutput, calls=%fused_computation.18 | convolution fusion | flops 541327360 | bytes 4726784 | tf_op jit(solution)/shard_map/dot_general | solution.py:122
  (116 shorter events, 31.7 us)
Async XLA Ops:
  6.5 91.3 %copy-start = (bf16[1024,128]{1,0:T(8,128)(2,1)S(1)}, bf16[1024,128]{1,0:T(8,128)(2,1)}, u32[]{:S(2)}) copy-start(bf16[1024,128]{1,0:T(8,128)(2,1)} %param.20) | copy-start | bytes 786436
  6.5 122.1 %all-gather.10.cloned.1.call-start = ((), (), s32[]{:S(2)}) async-start(), calls=%async_computation.5 | async-start | bytes 2359296 | tf_op jit(solution)/shard_map/all_gather | solution.py:78
  21.9 7.2 %copy-start.6 = (bf16[1024,128]{1,0:T(8,128)(2,1)S(1)}, bf16[1024,128]{1,0:T(8,128)(2,1)}, u32[]{:S(2)}) copy-start(bf16[1024,128]{1,0:T(8,128)(2,1)} %param.19) | copy-start | bytes 786436
  35.5 24.4 %copy-start.13 = (u32[32]{0:T(128)S(1)}, u32[32]{0:T(128)}, u32[]{:S(2)}) copy-start(u32[32]{0:T(128)} %constant.54) | copy-start | bytes 388
  57.4 20.5 %copy-start.3 = (bf16[1024,1024]{1,0:T(8,128)(2,1)S(1)}, bf16[1024,1024]{1,0:T(8,128)(2,1)}, u32[]{:S(2)}) copy-start(bf16[1024,1024]{1,0:T(8,128)(2,1)} %param.22) | copy-start | bytes 6291460
  58.3 166.2 %all-gather.6.cloned.1.call-start = ((), (), s32[]{:S(2)}) async-start(), calls=%async_computation.2 | async-start | bytes 7077888 | tf_op jit(solution)/shard_map/all_gather | solution.py:109
  59.0 165.5 %all-gather.8.cloned.1.call-start = ((), (), s32[]{:S(2)}) async-start(), calls=%async_computation.3 | async-start | bytes 7077888 | tf_op jit(solution)/shard_map/all_gather | solution.py:115
  59.8 218.2 %reduce-scatter.2.cloned.1.call-start = ((), (), s32[]{:S(2)}) async-start(), calls=%async_computation.4 | async-start | bytes 2621440 | tf_op jit(solution)/shard_map/reduce_scatter | solution.py:118
  92.2 5.4 %copy-start.10 = (f32[16]{0:T(128)S(1)}, f32[16]{0:T(128)}, u32[]{:S(2)}) copy-start(f32[16]{0:T(128)} %param.21) | copy-start | bytes 196
  92.2 5.7 %copy-start.8 = (f32[16,1024]{1,0:T(8,128)S(1)}, f32[16,1024]{1,0:T(8,128)}, u32[]{:S(2)}) copy-start(f32[16,1024]{1,0:T(8,128)} %param.17) | copy-start | bytes 196612
  92.2 5.7 %copy-start.7 = (bf16[1024,128]{1,0:T(8,128)(2,1)S(1)}, bf16[1024,128]{1,0:T(8,128)(2,1)}, u32[]{:S(2)}) copy-start(bf16[1024,128]{1,0:T(8,128)(2,1)} %param.19) | copy-start | bytes 786436
  98.2 12.5 %copy-start.2 = (f32[8,128,16,64]{1,3,2,0:T(8,128)S(1)}, f32[8,128,16,64]{1,3,2,0:T(8,128)}, u32[]{:S(2)}) copy-start(f32[8,128,16,64]{1,3,2,0:T(8,128)} %copy.76) | copy-start | bytes 12582916
  157.7 5.4 %copy-start.9 = (f32[1024]{0:T(1024)S(1)}, f32[1024]{0:T(1024)}, u32[]{:S(2)}) copy-start(f32[1024]{0:T(1024)} %param.23) | copy-start | bytes 12292
  163.1 8.3 %copy-start.11 = (s32[1024]{0:T(1024)S(1)}, s32[1024]{0:T(1024)}, u32[]{:S(2)}) copy-start(s32[1024]{0:T(1024)} %param.26) | copy-start | bytes 12292
  170.1 1.3 copy-start.4
  224.5 53.5 %copy-start.5 = (bf16[1024,1024]{1,0:T(8,128)(2,1)S(1)}, bf16[1024,1024]{1,0:T(8,128)(2,1)}, u32[]{:S(2)}) copy-start(bf16[1024,1024]{1,0:T(8,128)(2,1)} %copy-done.4) | copy-start | bytes 6291460
  224.5 53.5 %copy-start.12 = (f32[1024]{0:T(1024)S(1)}, f32[1024]{0:T(1024)}, u32[]{:S(2)}) copy-start(f32[1024]{0:T(1024)} %param.27) | copy-start | bytes 12292
  224.5 56.7 %copy-start.1 = (bf16[1024,128]{1,0:T(8,128)(2,1)S(1)}, bf16[1024,128]{1,0:T(8,128)(2,1)}, u32[]{:S(2)}) copy-start(bf16[1024,128]{1,0:T(8,128)(2,1)} %param.20) | copy-start | bytes 786436
Sparse Core Ops, SparseCore 0:
  58.4 30.5 all-gather.9
  90.9 45.3 all-gather.5
  138.2 46.5 all-gather.7
  236.0 41.9 reduce-scatter.1
